TPU v7x, 32 devices: a whole 2x2x4 slice. The times are simulated.
32 devices in a mesh: req: 8 (over z, y), ctx: 4 (over x, core).
Axes of the slice: x: 2, y: 2, z: 4, core: 2. Of those that a mesh axis runs over, the one named last changes fastest.
Arguments:
- history: bfloat16 [24576, 1024], P(('req', 'ctx')), may hold values from -6 to 6
- block_owner: int32 [1536, 1], P(('req', 'ctx')), may hold values from 0 to 7; in each aligned block of 48 rows (0 to 47, 48 to 95, ...) at most 12 rows name the same one
- candidates: bfloat16 [4096, 1024], P(('req', 'ctx')), may hold values from -6 to 6
- w_kv: bfloat16 [1024, 2048], replicated, may hold values from -0.1875 to 0.1875
- w_qu: bfloat16 [1024, 2048], replicated, may hold values from -0.1875 to 0.1875
- w_out: bfloat16 [1024, 1024], replicated, may hold values from -0.1875 to 0.1875
Outputs:
- scored: bfloat16 [4096, 1024], P(('req', 'ctx'))
Inputs may be any that keep to these rules, and one draw needn't show every extreme that they name: `block_owner`: each packed block belongs to one request; among the 48 blocks of one device at most 12 belong to the same request, and that most is reached on some device; every request owns at least one block.
All inputs are finite; a program needn't handle non-finite values.
Results may differ from a plain program's by a relative error of at most 0.0052.
Values may be sent and summed in bfloat16 or wider, within the bound.
No kernel may reach another device: no remote copies, remote signals or barrier semaphores. Data moves between devices by JAX's collectives and lax.ppermute only.
A program may use at most 128 MiB of HBM per device.

v0:
```python
import jax
import jax.numpy as jnp
from jax import lax
from jax.sharding import PartitionSpec as P

HEAD = 128
key_span = 512


def attend(queries, keys_values):
    count, width = queries.shape
    heads = width // HEAD
    rows = keys_values.shape[0]
    query = queries.reshape(count, heads, HEAD)
    pieces = keys_values.reshape(rows // key_span, key_span, 2, heads, HEAD)
    factor = HEAD ** (-0.5)

    def add_block(total, piece):
        scores = (
            jnp.einsum("qhd,khd->hqk", query, piece[:, 0], preferred_element_type=jnp.float32)
            * factor
        )
        weights = jax.nn.silu(scores).astype(jnp.bfloat16)
        return (
            total
            + jnp.einsum("hqk,khd->qhd", weights, piece[:, 1], preferred_element_type=jnp.float32),
            None,
        )

    total, _ = lax.scan(add_block, jnp.zeros((count, heads, HEAD), jnp.float32), pieces)
    return total.reshape(count, width)


def on_device(history, block_owner, candidates, w_kv, w_qu, w_out):
    owners_count = lax.axis_size("req")
    rows, width = history.shape
    blocks = block_owner.shape[0]
    events = rows // blocks
    capacity = 2 * blocks // owners_count
    owner = block_owner[:, 0]
    onehot = (owner[:, None] == jnp.arange(owners_count, dtype=jnp.int32)[None, :]).astype(
        jnp.int32
    )
    rank = jnp.sum((jnp.cumsum(onehot, axis=0) - onehot) * onehot, axis=1)
    slot = owner * capacity + rank
    placing = (
        slot[None, :] == jnp.arange(owners_count * capacity, dtype=jnp.int32)[:, None]
    ).astype(jnp.bfloat16)
    packed = jnp.dot(
        placing, history.reshape(blocks, events * width), preferred_element_type=jnp.float32
    )
    packed = packed.astype(jnp.bfloat16).reshape(owners_count, capacity, events, width)
    raw = lax.all_to_all(packed, "req", split_axis=0, concat_axis=0, tiled=True)
    flat = raw.reshape(-1, raw.shape[-1])
    linear = jnp.dot(flat, w_kv, preferred_element_type=jnp.float32)
    half = linear.shape[-1] // 2
    made = jnp.concatenate([jax.nn.silu(linear[:, :half]), linear[:, half:]], axis=1).astype(
        jnp.bfloat16
    )
    arrived = made.reshape(raw.shape[:-1] + (made.shape[-1],))
    context = arrived.reshape(-1, 2 * width)
    projected = jnp.dot(candidates, w_qu, preferred_element_type=jnp.float32)
    queries = jax.nn.silu(projected[:, :width]).astype(jnp.bfloat16)
    gate = jax.nn.silu(projected[:, width:])
    partial_value = attend(lax.all_gather(queries, "ctx", axis=0, tiled=True), context)
    attended = lax.psum_scatter(partial_value, "ctx", scatter_dimension=0, tiled=True)
    mean = jnp.mean(attended, axis=-1, keepdims=True)
    centred = attended - mean
    variance = jnp.mean(centred * centred, axis=-1, keepdims=True)
    mixed = (centred * lax.rsqrt(variance + 1e-05) * gate).astype(jnp.bfloat16)
    result = candidates.astype(jnp.float32) + jnp.dot(
        mixed, w_out, preferred_element_type=jnp.float32
    )
    return result.astype(jnp.bfloat16)


def solution(mesh):
    placed = (
        P(("req", "ctx"), None),
        P(("req", "ctx"), None),
        P(("req", "ctx"), None),
        P(),
        P(),
        P(),
    )
    return jax.shard_map(
        on_device, mesh=mesh, in_specs=placed, out_specs=P(("req", "ctx"), None), check_vma=False
    )
```

profile of v0, /device:TPU:0, one launch (start us, length us, event | category | flops | bytes accessed | tf_op | source)
XLA Modules:
  0.0 196.9 jit_solution(2472412631401539334)
XLA Ops:
  6.5 0.0 copy-start
  6.5 0.9 fusion.17
  7.4 0.1 reduce_window_sum.11
  7.5 0.8 select_reduce_fusion
  8.3 0.7 multiply_add_fusion
  9.0 3.8 %reshape.37 = bf16[48,16384]{1,0:T(8,128)(2,1)} reshape(bf16[768,1024]{1,0:T(8,128)(2,1)} %param.8) | data formatting | bytes 3145728 | tf_op jit(solution)/shard_map/reshape | solution.py:50
  12.8 2.4 %convolution_convert_fusion = bf16[96,16384]{1,0:T(8,128)(2,1)S(1)} fusion(bf16[48,16384]{1,0:T(8,128)(2,1)} %reshape.37, s32[48]{0:T(128)S(1)} %multiply_add_fusion), kind=kOutput, calls=%fused_computation.15 | convolution fusion | flops 152572416 | bytes 4718784 | tf_op jit(solution)/shard_map/dot_general | solution.py:49
  15.1 3.7 %copy.17 = bf16[12,8,16,1024]{3,2,1,0:T(8,128)(2,1)} copy(bf16[12,8,16,1024]{3,1,2,0:T(8,128)(2,1)S(1)} %bitcast.66) | data formatting | bytes 6291456
  18.8 0.0 copy-start.1
  18.8 7.4 %all-to-all-start = ((bf16[8,12,16,1024]{3,2,1,0:T(8,128)(2,1)}), bf16[8,12,16,1024]{3,2,1,0:T(8,128)(2,1)}, u32[]{:S(2)}, u32[]{:S(2)}) async-start(bf16[8,12,16,1024]{3,2,1,0:T(8,128)(2,1)} %bitcast.65), calls=%async_computation | async-start | bytes 6291456 | tf_op jit(solution)/shard_map/all_to_all | solution.py:53
  26.2 0.0 all-gather.2.cloned.1.call-start
  26.3 0.0 copy-done.1
  26.3 2.9 %fusion.20 = f32[128,2048]{1,0:T(8,128)S(1)} fusion(bf16[128,1024]{1,0:T(8,128)(2,1)S(1)} %copy-done.1, bf16[1024,2048]{1,0:T(8,128)(2,1)} %param.12), kind=kOutput, calls=%fused_computation.38 | convolution fusion | flops 536870912 | bytes 5505024 | tf_op jit(solution)/shard_map/dot_general | solution.py:62
  29.2 0.8 multiply_convert_fusion.2
  30.0 0.0 all-gather.2.cloned.1.call-update
  30.1 0.0 reduce-scatter.2.cloned.1.call-start
  30.1 18.2 %all-gather.2.cloned.1.call-done = bf16[512,1024]{1,0:T(8,128)(2,1)} async-done(((bf16[128,1024]{1,0:T(8,128)(2,1)}), bf16[512,1024]{1,0:T(8,128)(2,1)}) %all-gather.2.cloned.1.call-update) | async-done | bytes 1048592 | tf_op jit(solution)/shard_map/all_gather | solution.py:65
  48.3 2.4 %copy_bitcast_fusion.1 = bf16[512,8,128]{2,0,1:T(8,128)(2,1)} fusion(bf16[512,1024]{1,0:T(8,128)(2,1)} %all-gather.2.cloned.1.call-done), kind=kLoop, calls=%fused_computation.21 | loop fusion | bytes 2097152
  50.7 46.4 %all-to-all-done = bf16[8,12,16,1024]{3,2,1,0:T(8,128)(2,1)} async-done(((bf16[8,12,16,1024]{3,2,1,0:T(8,128)(2,1)}), bf16[8,12,16,1024]{3,2,1,0:T(8,128)(2,1)}, u32[]{:S(2)}, u32[]{:S(2)}) %all-to-all-start) | async-done | bytes 3145760 | tf_op jit(solution)/shard_map/all_to_all | solution.py:53
  97.0 9.5 %fusion.19 = f32[1536,2048]{1,0:T(8,128)S(1)} fusion(bf16[1536,1024]{1,0:T(8,128)(2,1)} %bitcast.1, bf16[1024,2048]{1,0:T(8,128)(2,1)} %param.11), kind=kOutput, calls=%fused_computation.37 | convolution fusion | flops 6442450944 | bytes 19922944 | tf_op jit(solution)/shard_map/dot_general | solution.py:55
  106.6 2.9 %multiply_convert_fusion = bf16[1536,1024]{1,0:T(8,128)(2,1)} fusion(f32[1536,2048]{1,0:T(8,128)S(1)} %fusion.19), kind=kLoop, calls=%fused_computation.18 | loop fusion | flops 7864320 | bytes 9437184 | tf_op jit(solution)/shard_map/convert
  109.5 0.5 slice.41
  110.0 3.9 %maximum_bitcast_fusion = bf16[192,8,16,128]{3,1,2,0:T(8,128)(2,1)S(1)} fusion(bf16[1536,1024]{1,0:T(8,128)(2,1)S(1)} %slice.41, bf16[1536,1024]{1,0:T(8,128)(2,1)} %multiply_convert_fusion), kind=kLoop, calls=%fused_computation.17 | loop fusion | flops 12582912 | bytes 12582912
  113.9 5.0 %copy.18 = bf16[192,8,16,128]{3,2,1,0:T(8,128)(2,1)} copy(bf16[192,8,16,128]{3,1,2,0:T(8,128)(2,1)S(1)} %maximum_bitcast_fusion) | data formatting | bytes 12582912
  118.9 33.1 %while.11 = (s32[]{:T(128)}, f32[512,8,128]{0,2,1:T(8,128)}, bf16[3,512,2,8,128]{4,3,2,1,0:T(8,128)(2,1)}, bf16[512,8,128]{2,0,1:T(8,128)(2,1)}, s32[]{:T(128)}, /*index=5*/s32[]{:T(128)}) while((s32[]{:T(128)}, f32[512,8,128]{0,2,1:T(8,128)}, bf16[3,512,2,8,128]{4,3,2,1,0:T(8,128)(2,1)}, bf16[512,8,128]{2,0,1:T(8,128)(2,1)}, ...), condition=%wide.region_3.4_spmd.clone, body=%wide.region_2.3_spmd.clone.sunk | while | flops 1087373312 | bytes 15728723 | solution.py:30
  118.9 2.0 constant_dynamic-slice_fusion.2
  120.9 1.9 copy.23
  122.8 6.7 %bitcast_add_fusion.2 = f32[512,8,128]{0,2,1:T(8,128)} fusion(f32[512,8,128]{0,2,1:T(8,128)} %get-tuple-element.87, bf16[512,8,128]{2,0,1:T(8,128)(2,1)} %get-tuple-element.95, bf16[512,2,8,128]{3,0,2,1:T(8,128)(2,1)} %bitcast.63, pred[]{:T(512)S(6)} %compare.3), kind=kOutput, calls=%fused_computation.9.clone.1 | convolution fusion | flops 1087373312 | bytes 7340033 | tf_op jit(solution)/shard_map/while/body/eval_jaxpr/hqk,khd->qhd/dot_general | solution.py:26
  129.5 2.0 constant_dynamic-slice_fusion.2
  131.4 1.9 copy.23
  133.3 7.4 %bitcast_add_fusion.2 = f32[512,8,128]{0,2,1:T(8,128)} fusion(f32[512,8,128]{0,2,1:T(8,128)} %get-tuple-element.87, bf16[512,8,128]{2,0,1:T(8,128)(2,1)} %get-tuple-element.95, bf16[512,2,8,128]{3,0,2,1:T(8,128)(2,1)} %bitcast.63, pred[]{:T(512)S(6)} %compare.3), kind=kOutput, calls=%fused_computation.9.clone.1 | convolution fusion | flops 1087373312 | bytes 7340033 | tf_op jit(solution)/shard_map/while/body/eval_jaxpr/hqk,khd->qhd/dot_general | solution.py:26
  140.7 2.0 constant_dynamic-slice_fusion.2
  142.7 1.9 copy.23
  144.6 7.4 %bitcast_add_fusion.2 = f32[512,8,128]{0,2,1:T(8,128)} fusion(f32[512,8,128]{0,2,1:T(8,128)} %get-tuple-element.87, bf16[512,8,128]{2,0,1:T(8,128)(2,1)} %get-tuple-element.95, bf16[512,2,8,128]{3,0,2,1:T(8,128)(2,1)} %bitcast.63, pred[]{:T(512)S(6)} %compare.3), kind=kOutput, calls=%fused_computation.9.clone.1 | convolution fusion | flops 1087373312 | bytes 7340033 | tf_op jit(solution)/shard_map/while/body/eval_jaxpr/hqk,khd->qhd/dot_general | solution.py:26
  152.0 2.9 %copy.14 = f32[512,1024]{1,0:T(8,128)} copy(f32[512,1024]{0,1:T(8,128)} %bitcast.67) | data formatting | bytes 4194304 | tf_op jit(solution)/shard_map/reshape | solution.py:31
  154.9 0.0 reduce-scatter.2.cloned.1.call-update
  154.9 30.4 %reduce-scatter.2.cloned.1.call-done = f32[128,1024]{1,0:T(8,128)} async-done(((f32[512,1024]{1,0:T(8,128)}), f32[128,1024]{1,0:T(8,128)}) %reduce-scatter.2.cloned.1.call-update) | async-done | bytes 524304 | tf_op jit(solution)/shard_map/reduce_scatter | solution.py:66
  185.3 1.2 reduce_sum.28
  186.5 1.2 multiply_reduce_fusion
  187.7 0.0 copy-done
  187.7 2.3 %fusion.12 = bf16[128,1024]{1,0:T(8,128)(2,1)} fusion(bf16[1024,1024]{1,0:T(8,128)(2,1)S(1)} %copy-done, bf16[128,1024]{1,0:T(8,128)(2,1)S(1)} %copy-done.1, f32[128,2048]{1,0:T(8,128)S(1)} %fusion.20, f32[128,1024]{1,0:T(8,128)} %reduce-scatter.2.cloned.1.call-done, f32[128]{0:T(128)S(1)} %add_rsqrt_fusion, f32[128]{0:T(128)S(1)} %broadcast_multiply_fusion), kind=kOutput, calls=%fused_computation.20 | convolution fusion | flops 269877248 | bytes 3671040 | tf_op jit(solution)/shard_map/dot_general | solution.py:71
  (3 shorter events, 0.0 us)
Async XLA Ops:
  6.5 181.2 %copy-start = (bf16[1024,1024]{1,0:T(8,128)(2,1)S(1)}, bf16[1024,1024]{1,0:T(8,128)(2,1)}, u32[]{:S(2)}) copy-start(bf16[1024,1024]{1,0:T(8,128)(2,1)} %param.13) | copy-start | bytes 6291460
  18.8 7.5 %copy-start.1 = (bf16[128,1024]{1,0:T(8,128)(2,1)S(1)}, bf16[128,1024]{1,0:T(8,128)(2,1)}, u32[]{:S(2)}) copy-start(bf16[128,1024]{1,0:T(8,128)(2,1)} %param.10) | copy-start | bytes 786436
  18.8 78.3 %all-to-all-start = ((bf16[8,12,16,1024]{3,2,1,0:T(8,128)(2,1)}), bf16[8,12,16,1024]{3,2,1,0:T(8,128)(2,1)}, u32[]{:S(2)}, u32[]{:S(2)}) async-start(bf16[8,12,16,1024]{3,2,1,0:T(8,128)(2,1)} %bitcast.65), calls=%async_computation | async-start | bytes 6291456 | tf_op jit(solution)/shard_map/all_to_all | solution.py:53
  26.2 22.1 %all-gather.2.cloned.1.call-start = ((), (), s32[]{:S(2)}) async-start(), calls=%async_computation.2 | async-start | bytes 1310720 | tf_op jit(solution)/shard_map/all_gather | solution.py:65
  30.1 155.2 %reduce-scatter.2.cloned.1.call-start = ((), (), s32[]{:S(2)}) async-start(), calls=%async_computation.3 | async-start | bytes 2621440 | tf_op jit(solution)/shard_map/reduce_scatter | solution.py:66
Sparse Core Ops, SparseCore 0:
  30.2 18.0 all-gather.1
  155.1 30.1 reduce-scatter.1
where the time goes:
time: 198 us; the launch traced here: 197 us
  waiting for transfers between devices  94.9 us (48%)
  matrix products  38.5 us (19%)
  local copies, waits for them, and re-layouts  29.9 us (15%)
  between operations  13.5 us (7%)
  other arithmetic  12.5 us (6%)
  starting transfers between devices  7.52 us (4%)
    all_to_all x1, waiting for transfers between devices, on_device(): raw = lax.all_to_all(packed, 'req', split_axis=0, concat_axis=0, tiled=True)  46.4 us
    reduce_scatter x1, waiting for transfers between devices, on_device(): lax.psum_scatter(partial_value, 'ctx', scatter_dimension=0, tiled=True)  30.4 us
    dot_general x3, matrix products, add_block(): jnp.einsum('hqk,khd->qhd', weights, piece[:, 1], preferred_element_type=j...  21.4 us
    all_gather x1, waiting for transfers between devices, on_device(): lax.all_gather(queries, 'ctx', axis=0, tiled=True)  18.2 us
    dynamic_slice x6, local copies, waits for them, and re-layouts, attend(): lax.scan(add_block, jnp.zeros((count, heads, HEAD), jnp.float32), pieces)  11.7 us
    unnamed x7, local copies, waits for them, and re-layouts  11.1 us
    dot_general x1, matrix products, on_device(): linear = jnp.dot(flat, w_kv, preferred_element_type=jnp.float32)  9.53 us
    all_to_all x1, starting transfers between devices, on_device(): raw = lax.all_to_all(packed, 'req', split_axis=0, concat_axis=0, tiled=True)  7.44 us
  transfers between devices with their start and end apart: 3, of which 3 were waited for; matrix products, arithmetic and copies ran while one was open for 3% of the time, Pallas kernels for 0%

commit v1 on v0

--- a/solution.py
+++ b/solution.py
@@ -5,6 +5,29 @@
 
 HEAD = 128
 key_span = 512
+
+
+def cut_along(x, dim, size):
+    dims = x.shape
+    tiles = x.reshape(*dims[:dim], size, dims[dim] // size, *dims[dim + 1 :])
+    return jnp.moveaxis(tiles, dim, 0)
+
+
+def laid_out(blocks, dim):
+    shape = list(blocks.shape[1:])
+    shape[dim] *= blocks.shape[0]
+    return jnp.moveaxis(blocks, 0, dim).reshape(shape)
+
+
+def exchange_in_pairs(array, axis, split_dim, concat_dim):
+    peers, index = (lax.axis_size(axis), lax.axis_index(axis))
+    parts = cut_along(array, split_dim, peers)
+    finished = [parts[index]]
+    for step in range(1, peers):
+        sent = parts[index ^ step]
+        finished.append(lax.ppermute(sent, axis, [(i, i ^ step) for i in range(peers)]))
+    parts = jnp.stack(finished)[index ^ jnp.arange(peers)]
+    return laid_out(parts, concat_dim)
 
 
 def attend(queries, keys_values):
@@ -50,7 +73,7 @@
         placing, history.reshape(blocks, events * width), preferred_element_type=jnp.float32
     )
     packed = packed.astype(jnp.bfloat16).reshape(owners_count, capacity, events, width)
-    raw = lax.all_to_all(packed, "req", split_axis=0, concat_axis=0, tiled=True)
+    raw = exchange_in_pairs(packed, "req", 0, 0)
     flat = raw.reshape(-1, raw.shape[-1])
     linear = jnp.dot(flat, w_kv, preferred_element_type=jnp.float32)
     half = linear.shape[-1] // 2

time: 198 us -> 207 us (1.045)
  local copies, waits for them, and re-layouts: 29.9 us -> 47.3 us
  waiting for transfers between devices: 94.9 us -> 82.7 us
  starting transfers between devices: 7.52 us -> 13.7 us
  matrix products: 38.5 us -> 36.3 us
    all_to_all x1 -> x0, waiting for transfers between devices: 46.4 us -> none  [on_device(): raw = lax.all_to_all(packed, 'req', split_axis=0, concat_axis=0, tiled=True)]
    ppermute x0 -> x7, waiting for transfers between devices: none -> 38.7 us  [exchange_in_pairs(): lax.ppermute(sent, axis, [(i, i ^ step) for i in range(peers)])]
    all_gather x1, waiting for transfers between devices: 18.2 us -> 0.01 us  [on_device(): lax.all_gather(queries, 'ctx', axis=0, tiled=True)]
    reduce_scatter x1, waiting for transfers between devices: 30.4 us -> 44 us  [on_device(): lax.psum_scatter(partial_value, 'ctx', scatter_dimension=0, tiled=True)]
    ppermute x0 -> x7, starting transfers between devices: none -> 13.6 us  [exchange_in_pairs(): lax.ppermute(sent, axis, [(i, i ^ step) for i in range(peers)])]
    unnamed x7 -> x17, local copies, waits for them, and re-layouts: 11.1 us -> 19.8 us
    all_to_all x1 -> x0, starting transfers between devices: 7.44 us -> none  [on_device(): raw = lax.all_to_all(packed, 'req', split_axis=0, concat_axis=0, tiled=True)]
    gather x0 -> x1, local copies, waits for them, and re-layouts: none -> 4.31 us  [exchange_in_pairs(): parts = jnp.stack(finished)[index ^ jnp.arange(peers)]]
  transfers between devices with their start and end apart: 3 -> 9, of which waited for: 3 -> 5; matrix products, arithmetic and copies ran while one was open for 3% -> 18% of each run, Pallas kernels for 0% -> 0%
where the time goes in v1:
time: 207 us; the launch traced here: 206 us
  waiting for transfers between devices  82.7 us (40%)
  local copies, waits for them, and re-layouts  47.3 us (23%)
  matrix products  36.3 us (18%)
  starting transfers between devices  13.7 us (7%)
  between operations  13.5 us (7%)
  other arithmetic  12.5 us (6%)
    reduce_scatter x1, waiting for transfers between devices, on_device(): lax.psum_scatter(partial_value, 'ctx', scatter_dimension=0, tiled=True)  44 us
    ppermute x7, waiting for transfers between devices, exchange_in_pairs(): lax.ppermute(sent, axis, [(i, i ^ step) for i in range(peers)])  38.7 us
    dot_general x3, matrix products, add_block(): jnp.einsum('hqk,khd->qhd', weights, piece[:, 1], preferred_element_type=j...  21.4 us
    unnamed x17, local copies, waits for them, and re-layouts  19.8 us
    ppermute x7, starting transfers between devices, exchange_in_pairs(): lax.ppermute(sent, axis, [(i, i ^ step) for i in range(peers)])  13.6 us
    dynamic_slice x6, local copies, waits for them, and re-layouts, attend(): lax.scan(add_block, jnp.zeros((count, heads, HEAD), jnp.float32), pieces)  11.5 us
    dot_general x1, matrix products, on_device(): linear = jnp.dot(flat, w_kv, preferred_element_type=jnp.float32)  9.53 us
    gather x1, local copies, waits for them, and re-layouts, exchange_in_pairs(): parts = jnp.stack(finished)[index ^ jnp.arange(peers)]  4.31 us
  transfers between devices with their start and end apart: 9, of which 5 were waited for; matrix products, arithmetic and copies ran while one was open for 18% of the time, Pallas kernels for 0%

profile of v1, /device:TPU:0, one launch (start us, length us, event | category | flops | bytes accessed | tf_op | source)
XLA Modules:
  0.0 206.1 jit_solution(2067396917091008070)
XLA Ops:
  6.5 0.0 copy-start
  6.5 0.0 all-gather.2.cloned.1.call-start
  6.5 0.9 fusion.17
  7.4 0.1 reduce_window_sum.11
  7.5 0.8 select_reduce_fusion
  8.3 0.7 multiply_add_fusion
  9.0 3.8 %reshape.47 = bf16[48,16384]{1,0:T(8,128)(2,1)} reshape(bf16[768,1024]{1,0:T(8,128)(2,1)} %param.8) | data formatting | bytes 3145728 | tf_op jit(solution)/shard_map/reshape | solution.py:73
  12.8 2.4 %convolution_convert_fusion = bf16[96,16384]{1,0:T(8,128)(2,1)S(1)} fusion(bf16[48,16384]{1,0:T(8,128)(2,1)} %reshape.47, s32[48]{0:T(128)S(1)} %multiply_add_fusion), kind=kOutput, calls=%fused_computation.16 | convolution fusion | flops 152572416 | bytes 4718784 | tf_op jit(solution)/shard_map/dot_general | solution.py:72
  15.1 3.6 %copy.17 = bf16[12,8,16,1024]{3,2,1,0:T(8,128)(2,1)} copy(bf16[12,8,16,1024]{3,1,2,0:T(8,128)(2,1)S(1)} %bitcast.97) | data formatting | bytes 6291456
  18.8 0.0 copy-start.1
  18.8 3.7 %dynamic-slice_bitcast_fusion = (bf16[1,12,16,1024]{3,2,1,0:T(8,128)(2,1)}, bf16[1,12,16,1024]{3,2,1,0:T(8,128)(2,1)}, bf16[1,12,16,1024]{3,2,1,0:T(8,128)(2,1)}...) fusion(bf16[8,1,12,16,1024]{4,3,2,0,1:T(8,128)(2,1)} %bitcast.9, ...), kind=kLoop, calls=%fused_computation.33 | loop fusion | bytes 6291488 | tf_op jit(solution)/shard_map/squeeze | solution.py:27
  22.5 3.0 %collective-permute-start = (bf16[1,12,16,1024]{3,2,1,0:T(8,128)(2,1)}, bf16[1,12,16,1024]{3,2,1,0:T(8,128)(2,1)}, u32[]{:S(2)}, u32[]{:S(2)}) collective-permute-start(bf16[1,12,16,1024]{3,2,1,0:T(8,128)(2,1)} %get-tuple-element.61), channel_id=1, source_target_pairs={{0,4},{4,0},{8,12},{12,8},{16,20},{20,16},{24,28},{28,24},{1,5},{5... | collective-permute-start | bytes 1179656 | tf_op jit(solution)/shard_map/ppermute | solution.py:28
  25.5 1.6 collective-permute-start.1
  27.0 0.0 collective-permute-start.2
  27.0 3.0 %collective-permute-start.3 = (bf16[1,12,16,1024]{3,2,1,0:T(8,128)(2,1)}, bf16[1,12,16,1024]{3,2,1,0:T(8,128)(2,1)}, u32[]{:S(2)}, u32[]{:S(2)}) collective-permute-start(bf16[1,12,16,1024]{3,2,1,0:T(8,128)(2,1)} %get-tuple-element.58), channel_id=1, source_target_pairs={{0,16},{4,20},{8,24},{12,28},{16,0},{20,4},{24,8},{28,12},{1,17},{... | collective-permute-start | bytes 1179656 | tf_op jit(solution)/shard_map/ppermute | solution.py:28
  30.0 1.3 collective-permute-start.4
  31.3 0.0 copy-done.1
  31.3 0.0 copy-done.2
  31.3 0.7 fusion.21
  32.0 0.8 multiply_convert_fusion.2
  32.9 0.0 all-gather.2.cloned.1.call-update
  32.9 0.0 reduce-scatter.2.cloned.1.call-start
  33.0 1.9 collective-permute-done
  34.9 3.8 %collective-permute-start.5 = (bf16[1,12,16,1024]{3,2,1,0:T(8,128)(2,1)}, bf16[1,12,16,1024]{3,2,1,0:T(8,128)(2,1)S(1)}, u32[]{:S(2)}, u32[]{:S(2)}) collective-permute-start(bf16[1,12,16,1024]{3,2,1,0:T(8,128)(2,1)} %get-tuple-element.56), channel_id=1, source_target_pairs={{0,24},{4,28},{8,16},{12,20},{16,8},{20,12},{24,0},{28,4},{1,25},{... | collective-permute-start | bytes 1179656 | tf_op jit(solution)/shard_map/ppermute | solution.py:28
  38.7 1.8 bitcast_dynamic-update-slice_fusion.6
  40.5 13.2 %collective-permute-done.1 = bf16[1,12,16,1024]{3,2,1,0:T(8,128)(2,1)} collective-permute-done((bf16[1,12,16,1024]{3,2,1,0:T(8,128)(2,1)}, bf16[1,12,16,1024]{3,2,1,0:T(8,128)(2,1)}, u32[]{:S(2)}, u32[]{:S(2)}) %collective-permute-start.1) | collective-permute-done | bytes 393248 | tf_op jit(solution)/shard_map/ppermute | solution.py:28
  53.7 1.0 collective-permute-start.6
  54.7 1.8 bitcast_dynamic-update-slice_fusion.5
  56.4 3.4 %collective-permute-done.2 = bf16[1,12,16,1024]{3,2,1,0:T(8,128)(2,1)} collective-permute-done((bf16[1,12,16,1024]{3,2,1,0:T(8,128)(2,1)}, bf16[1,12,16,1024]{3,2,1,0:T(8,128)(2,1)}, u32[]{:S(2)}, u32[]{:S(2)}) %collective-permute-start.2) | collective-permute-done | bytes 393248 | tf_op jit(solution)/shard_map/ppermute | solution.py:28
  59.8 1.8 bitcast_dynamic-update-slice_fusion.4
  61.6 0.0 collective-permute-done.3
  61.6 1.8 bitcast_dynamic-update-slice_fusion.3
  63.4 20.2 %collective-permute-done.4 = bf16[1,12,16,1024]{3,2,1,0:T(8,128)(2,1)S(1)} collective-permute-done((bf16[1,12,16,1024]{3,2,1,0:T(8,128)(2,1)}, bf16[1,12,16,1024]{3,2,1,0:T(8,128)(2,1)S(1)}, u32[]{:S(2)}, u32[]{:S(2)}) %collective-permute-start.4) | collective-permute-done | bytes 393248 | tf_op jit(solution)/shard_map/ppermute | solution.py:28
  83.6 0.8 bitcast_dynamic-update-slice_fusion.2
  84.4 0.0 collective-permute-done.5
  84.4 0.8 bitcast_dynamic-update-slice_fusion.1
  85.2 0.0 collective-permute-done.6
  85.2 0.8 bitcast_dynamic-update-slice_fusion
  86.0 4.3 %gather_fusion = bf16[8,12,16,1024]{3,2,1,0:T(8,128)(2,1)} fusion(bf16[8,12,16,1024]{3,2,1,0:T(8,128)(2,1)} %bitcast.99, s32[1024]{0:T(1024)S(1)} %pad_clamp_fusion), kind=kCustom, calls=%fused_computation | custom fusion | bytes 6291488 | tf_op jit(solution)/shard_map/gather | solution.py:29
  90.3 9.5 %fusion.20 = f32[1536,2048]{1,0:T(8,128)S(1)} fusion(bf16[1536,1024]{1,0:T(8,128)(2,1)} %bitcast.100, bf16[1024,2048]{1,0:T(8,128)(2,1)} %param.11), kind=kOutput, calls=%fused_computation.56 | convolution fusion | flops 6442450944 | bytes 19922944 | tf_op jit(solution)/shard_map/dot_general | solution.py:78
  99.9 0.5 slice.43
  100.4 2.9 %multiply_convert_fusion = bf16[1536,1024]{1,0:T(8,128)(2,1)} fusion(f32[1536,2048]{1,0:T(8,128)S(1)} %fusion.20), kind=kLoop, calls=%fused_computation.19 | loop fusion | flops 7864320 | bytes 9437184 | tf_op jit(solution)/shard_map/convert
  103.3 3.9 %maximum_bitcast_fusion = bf16[192,8,16,128]{3,1,2,0:T(8,128)(2,1)S(1)} fusion(bf16[1536,1024]{1,0:T(8,128)(2,1)S(1)} %slice.43, bf16[1536,1024]{1,0:T(8,128)(2,1)} %multiply_convert_fusion), kind=kLoop, calls=%fused_computation.18 | loop fusion | flops 12582912 | bytes 12582912
  107.2 5.0 %copy.18 = bf16[192,8,16,128]{3,2,1,0:T(8,128)(2,1)} copy(bf16[192,8,16,128]{3,1,2,0:T(8,128)(2,1)S(1)} %maximum_bitcast_fusion) | data formatting | bytes 12582912
  112.2 0.0 all-gather.2.cloned.1.call-done
  112.2 2.4 %copy_bitcast_fusion.1 = bf16[512,8,128]{2,0,1:T(8,128)(2,1)} fusion(bf16[512,1024]{1,0:T(8,128)(2,1)} %all-gather.2.cloned.1.call-done), kind=kLoop, calls=%fused_computation.22 | loop fusion | bytes 2097152
  114.6 32.9 %while.11 = (s32[]{:T(128)}, f32[512,8,128]{0,2,1:T(8,128)}, bf16[3,512,2,8,128]{4,3,2,1,0:T(8,128)(2,1)}, bf16[512,8,128]{2,0,1:T(8,128)(2,1)}, s32[]{:T(128)}, /*index=5*/s32[]{:T(128)}) while((s32[]{:T(128)}, f32[512,8,128]{0,2,1:T(8,128)}, bf16[3,512,2,8,128]{4,3,2,1,0:T(8,128)(2,1)}, bf16[512,8,128]{2,0,1:T(8,128)(2,1)}, ...), condition=%wide.region_3.4_spmd.clone, body=%wide.region_2.3_spmd.clone.sunk | while | flops 1087373312 | bytes 15728723 | solution.py:53
  114.6 2.0 constant_dynamic-slice_fusion.2
  116.5 1.9 copy.23
  118.4 6.7 %bitcast_add_fusion.2 = f32[512,8,128]{0,2,1:T(8,128)} fusion(f32[512,8,128]{0,2,1:T(8,128)} %get-tuple-element.95, bf16[512,8,128]{2,0,1:T(8,128)(2,1)} %get-tuple-element.103, bf16[512,2,8,128]{3,0,2,1:T(8,128)(2,1)} %bitcast.95, pred[]{:T(512)S(6)} %compare.3), kind=kOutput, calls=%fused_computation.10.clone.1 | convolution fusion | flops 1087373312 | bytes 7340033 | tf_op jit(solution)/shard_map/while/body/eval_jaxpr/hqk,khd->qhd/dot_general | solution.py:49
  125.1 2.0 constant_dynamic-slice_fusion.2
  127.1 1.9 copy.23
  129.0 7.4 %bitcast_add_fusion.2 = f32[512,8,128]{0,2,1:T(8,128)} fusion(f32[512,8,128]{0,2,1:T(8,128)} %get-tuple-element.95, bf16[512,8,128]{2,0,1:T(8,128)(2,1)} %get-tuple-element.103, bf16[512,2,8,128]{3,0,2,1:T(8,128)(2,1)} %bitcast.95, pred[]{:T(512)S(6)} %compare.3), kind=kOutput, calls=%fused_computation.10.clone.1 | convolution fusion | flops 1087373312 | bytes 7340033 | tf_op jit(solution)/shard_map/while/body/eval_jaxpr/hqk,khd->qhd/dot_general | solution.py:49
  136.3 2.0 constant_dynamic-slice_fusion.2
  138.3 1.9 copy.23
  140.2 7.4 %bitcast_add_fusion.2 = f32[512,8,128]{0,2,1:T(8,128)} fusion(f32[512,8,128]{0,2,1:T(8,128)} %get-tuple-element.95, bf16[512,8,128]{2,0,1:T(8,128)(2,1)} %get-tuple-element.103, bf16[512,2,8,128]{3,0,2,1:T(8,128)(2,1)} %bitcast.95, pred[]{:T(512)S(6)} %compare.3), kind=kOutput, calls=%fused_computation.10.clone.1 | convolution fusion | flops 1087373312 | bytes 7340033 | tf_op jit(solution)/shard_map/while/body/eval_jaxpr/hqk,khd->qhd/dot_general | solution.py:49
  147.5 3.0 %copy.14 = f32[512,1024]{1,0:T(8,128)} copy(f32[512,1024]{0,1:T(8,128)} %bitcast.101) | data formatting | bytes 4194304 | tf_op jit(solution)/shard_map/reshape | solution.py:54
  150.5 0.0 reduce-scatter.2.cloned.1.call-update
  150.5 44.0 %reduce-scatter.2.cloned.1.call-done = f32[128,1024]{1,0:T(8,128)} async-done(((f32[512,1024]{1,0:T(8,128)}), f32[128,1024]{1,0:T(8,128)}) %reduce-scatter.2.cloned.1.call-update) | async-done | bytes 524304 | tf_op jit(solution)/shard_map/reduce_scatter | solution.py:89
  194.5 1.2 reduce_sum.28
  195.7 1.2 multiply_reduce_fusion
  196.9 0.0 copy-done
  196.9 0.0 copy-done.3
  196.9 2.3 %fusion.12 = bf16[128,1024]{1,0:T(8,128)(2,1)} fusion(bf16[1024,1024]{1,0:T(8,128)(2,1)S(1)} %copy-done, bf16[128,1024]{1,0:T(8,128)(2,1)S(1)} %copy-done.3, f32[128,2048]{1,0:T(8,128)S(1)} %fusion.21, f32[128,1024]{1,0:T(8,128)} %reduce-scatter.2.cloned.1.call-done, f32[128]{0:T(128)S(1)} %add_rsqrt_fusion, f32[128]{0:T(128)S(1)} %broadcast_multiply_fusion), kind=kOutput, calls=%fused_computation.21 | convolution fusion | flops 269877248 | bytes 3671040 | tf_op jit(solution)/shard_map/dot_general | solution.py:94
  (7 shorter events, 0.0 us)
Async XLA Ops:
  6.5 190.4 %copy-start = (bf16[1024,1024]{1,0:T(8,128)(2,1)S(1)}, bf16[1024,1024]{1,0:T(8,128)(2,1)}, u32[]{:S(2)}) copy-start(bf16[1024,1024]{1,0:T(8,128)(2,1)} %param.13) | copy-start | bytes 6291460
  6.5 105.7 %all-gather.2.cloned.1.call-start = ((), (), s32[]{:S(2)}) async-start(), calls=%async_computation.1 | async-start | bytes 1310720 | tf_op jit(solution)/shard_map/all_gather | solution.py:88
  18.8 12.6 %copy-start.1 = (bf16[1024,2048]{1,0:T(8,128)(2,1)S(1)}, bf16[1024,2048]{1,0:T(8,128)(2,1)}, u32[]{:S(2)}) copy-start(bf16[1024,2048]{1,0:T(8,128)(2,1)} %param.12) | copy-start | bytes 12582916
  18.8 12.6 %copy-start.2 = (bf16[128,1024]{1,0:T(8,128)(2,1)S(1)}, bf16[128,1024]{1,0:T(8,128)(2,1)}, u32[]{:S(2)}) copy-start(bf16[128,1024]{1,0:T(8,128)(2,1)} %param.10) | copy-start | bytes 786436
  22.5 12.4 %collective-permute-start = (bf16[1,12,16,1024]{3,2,1,0:T(8,128)(2,1)}, bf16[1,12,16,1024]{3,2,1,0:T(8,128)(2,1)}, u32[]{:S(2)}, u32[]{:S(2)}) collective-permute-start(bf16[1,12,16,1024]{3,2,1,0:T(8,128)(2,1)} %get-tuple-element.61), channel_id=1, source_target_pairs={{0,4},{4,0},{8,12},{12,8},{16,20},{20,16},{24,28},{28,24},{1,5},{5... | collective-permute-start | bytes 1179656 | tf_op jit(solution)/shard_map/ppermute | solution.py:28
  25.5 28.2 %collective-permute-start.1 = (bf16[1,12,16,1024]{3,2,1,0:T(8,128)(2,1)}, bf16[1,12,16,1024]{3,2,1,0:T(8,128)(2,1)}, u32[]{:S(2)}, u32[]{:S(2)}) collective-permute-start(bf16[1,12,16,1024]{3,2,1,0:T(8,128)(2,1)} %get-tuple-element.60), channel_id=1, source_target_pairs={{0,8},{4,12},{8,0},{12,4},{16,24},{20,28},{24,16},{28,20},{1,9},{5... | collective-permute-start | bytes 1179656 | tf_op jit(solution)/shard_map/ppermute | solution.py:28
  27.0 32.8 %collective-permute-start.2 = (bf16[1,12,16,1024]{3,2,1,0:T(8,128)(2,1)}, bf16[1,12,16,1024]{3,2,1,0:T(8,128)(2,1)}, u32[]{:S(2)}, u32[]{:S(2)}) collective-permute-start(bf16[1,12,16,1024]{3,2,1,0:T(8,128)(2,1)} %get-tuple-element.59), channel_id=1, source_target_pairs={{0,12},{4,8},{8,4},{12,0},{16,28},{20,24},{24,20},{28,16},{1,13},{... | collective-permute-start | bytes 1179656 | tf_op jit(solution)/shard_map/ppermute | solution.py:28
  27.0 34.6 %collective-permute-start.3 = (bf16[1,12,16,1024]{3,2,1,0:T(8,128)(2,1)}, bf16[1,12,16,1024]{3,2,1,0:T(8,128)(2,1)}, u32[]{:S(2)}, u32[]{:S(2)}) collective-permute-start(bf16[1,12,16,1024]{3,2,1,0:T(8,128)(2,1)} %get-tuple-element.58), channel_id=1, source_target_pairs={{0,16},{4,20},{8,24},{12,28},{16,0},{20,4},{24,8},{28,12},{1,17},{... | collective-permute-start | bytes 1179656 | tf_op jit(solution)/shard_map/ppermute | solution.py:28
  30.0 53.6 %collective-permute-start.4 = (bf16[1,12,16,1024]{3,2,1,0:T(8,128)(2,1)}, bf16[1,12,16,1024]{3,2,1,0:T(8,128)(2,1)S(1)}, u32[]{:S(2)}, u32[]{:S(2)}) collective-permute-start(bf16[1,12,16,1024]{3,2,1,0:T(8,128)(2,1)} %get-tuple-element.57), channel_id=1, source_target_pairs={{0,20},{4,16},{8,28},{12,24},{16,4},{20,0},{24,12},{28,8},{1,21},{... | collective-permute-start | bytes 1179656 | tf_op jit(solution)/shard_map/ppermute | solution.py:28
  32.9 161.6 %reduce-scatter.2.cloned.1.call-start = ((), (), s32[]{:S(2)}) async-start(), calls=%async_computation.2 | async-start | bytes 2621440 | tf_op jit(solution)/shard_map/reduce_scatter | solution.py:89
  34.9 49.6 %collective-permute-start.5 = (bf16[1,12,16,1024]{3,2,1,0:T(8,128)(2,1)}, bf16[1,12,16,1024]{3,2,1,0:T(8,128)(2,1)S(1)}, u32[]{:S(2)}, u32[]{:S(2)}) collective-permute-start(bf16[1,12,16,1024]{3,2,1,0:T(8,128)(2,1)} %get-tuple-element.56), channel_id=1, source_target_pairs={{0,24},{4,28},{8,16},{12,20},{16,8},{20,12},{24,0},{28,4},{1,25},{... | collective-permute-start | bytes 1179656 | tf_op jit(solution)/shard_map/ppermute | solution.py:28
  53.7 31.5 %collective-permute-start.6 = (bf16[1,12,16,1024]{3,2,1,0:T(8,128)(2,1)}, bf16[1,12,16,1024]{3,2,1,0:T(8,128)(2,1)S(1)}, u32[]{:S(2)}, u32[]{:S(2)}) collective-permute-start(bf16[1,12,16,1024]{3,2,1,0:T(8,128)(2,1)} %get-tuple-element.55), channel_id=1, source_target_pairs={{0,28},{4,24},{8,20},{12,16},{16,12},{20,8},{24,4},{28,0},{1,29},{... | collective-permute-start | bytes 1179656 | tf_op jit(solution)/shard_map/ppermute | solution.py:28
  147.5 49.4 %copy-start.3 = (bf16[128,1024]{1,0:T(8,128)(2,1)S(1)}, bf16[128,1024]{1,0:T(8,128)(2,1)}, u32[]{:S(2)}) copy-start(bf16[128,1024]{1,0:T(8,128)(2,1)} %param.10) | copy-start | bytes 786436
Sparse Core Ops, SparseCore 0:
  33.0 16.9 all-gather.1
  150.6 43.8 reduce-scatter.1
